TPU v7x, 128 devices: a whole 4x4x4 slice. The times are simulated.
128 devices in a mesh: ctx: 8 (over y, x_hi), head: 16 (over x_lo, z, core).
Axes of the slice: x: 4 (x_hi: 2, x_lo: 2; x = x_hi * 2 + x_lo), y: 4, z: 4, core: 2. Of those that a mesh axis runs over, the one named last changes fastest.
Arguments:
- queries: bfloat16 [2, 4096, 4096], P(None, 'ctx', 'head'), may hold values from -6 to 6
- keys: bfloat16 [2, 4096, 4096], P(None, 'ctx', 'head'), may hold values from -6 to 6
- values: bfloat16 [2, 4096, 4096], P(None, 'ctx', 'head'), may hold values from -6 to 6
- rates: float32 [16, 2, 4096], P('head', None, 'ctx'), may hold values from 0.05 to 1
- w_gate: float32 [16, 256, 512], P('head'), may hold values from -0.375 to 0.375
- w_up: float32 [16, 256, 512], P('head'), may hold values from -0.375 to 0.375
- w_down: float32 [16, 512, 256], P('head'), may hold values from -0.25 to 0.25
- gains: float32 [16, 256], P('head'), may hold values from 0.25 to 0.6
- out_proj: bfloat16 [4096, 4096], P('head'), may hold values from -0.125 to 0.125
Outputs:
- output: bfloat16 [2, 4096, 4096], P(None, 'ctx', 'head')
All inputs are finite; a program needn't handle non-finite values.
Results may differ from a plain program's by a relative error of at most 0.0051.
Values may be sent and summed in bfloat16 or wider, within the bound.
A program may use at most 128 MiB of HBM per device.

v0:
```python
import jax
import jax.numpy as jnp
from jax import lax
from jax.sharding import PartitionSpec as P

WINDOW = 256
NS_ITERS = 5
highest = lax.Precision.HIGHEST
attn_temp = 5.0
step_size = 0.5
quintic_one = 3.4445
quintic_two = -4.775
quintic_three = 2.0315


def passed_along(value, axis, steps):
    count = lax.axis_size(axis)
    pairs = [(source, (source + steps) % count) for source in range(count)]
    return lax.ppermute(value, axis, pairs)


def unit_rows(matrix):
    return matrix / jnp.sqrt(jnp.sum(matrix * matrix, axis=-1, keepdims=True) + 1e-06)


def exact_dot(left, right):
    return jnp.dot(left, right, precision=highest, preferred_element_type=jnp.float32)


def fast_grads(key_unit, value_rows, rate_rows, w_gate, w_up, w_down):
    gate_pre = exact_dot(key_unit, w_gate)
    up_pre = exact_dot(key_unit, w_up)
    sigma = jax.nn.sigmoid(gate_pre)
    gate_act = gate_pre * sigma
    hidden = gate_act * up_pre
    target = rate_rows[:, None] * value_rows
    grad_down = exact_dot(hidden.T, target)
    back_hidden = exact_dot(target, w_down.T)
    slope = sigma * (1.0 + gate_pre * (1.0 - sigma))
    grad_gate = exact_dot(key_unit.T, back_hidden * up_pre * slope)
    grad_up = exact_dot(key_unit.T, back_hidden * gate_act)
    return jnp.stack([grad_gate, grad_up, grad_down.T])


def quintic_step(gram, iterate):
    poly = quintic_two * gram + quintic_three * jnp.einsum(
        "mij,mjk->mik", gram, gram, precision=highest
    )
    return quintic_one * iterate + jnp.einsum("mij,mjk->mik", poly, iterate, precision=highest)


def orthogonal(grads):
    norms = jnp.sqrt(jnp.sum(grads * grads, axis=(1, 2), keepdims=True)) + 1e-06
    iterate = grads / norms
    for sweep_at in range(NS_ITERS):
        gram = jnp.einsum("mik,mjk->mij", iterate, iterate, precision=highest)
        iterate = quintic_step(gram, iterate)
    return iterate


def apply_fast(query_unit, w_gate, w_up, w_down):
    gate_pre = exact_dot(query_unit, w_gate)
    gate_act = gate_pre * jax.nn.sigmoid(gate_pre)
    return exact_dot(gate_act * exact_dot(query_unit, w_up), w_down)


def band_attention(query_half, ext_keys, ext_values, masked_head):
    local_rows = query_half.shape[0]
    block_rows = min(512, local_rows)
    scores = lax.dot_general(
        query_half, ext_keys, (((1,), (1,)), ((), ())), preferred_element_type=jnp.float32
    )
    query_pos = jnp.arange(block_rows, dtype=jnp.int32)[:, None]
    key_pos = jnp.arange(block_rows + WINDOW, dtype=jnp.int32)[None, :]
    distance = query_pos + WINDOW - key_pos
    valid = (distance >= 0) & (distance < WINDOW)
    if masked_head is not None:
        valid = valid & ((key_pos + 0 >= WINDOW) | jnp.logical_not(masked_head))
    weights = jnp.where(valid, jnp.exp(attn_temp * (scores - 1.0)), 0.0)
    probs = (weights / jnp.sum(weights, axis=-1, keepdims=True)).astype(jnp.bfloat16)
    outputs = jnp.dot(probs, ext_values, preferred_element_type=jnp.float32)
    return outputs


def body(queries, keys, values, rates, w_gate, w_up, w_down, gains, out_proj):
    group_count, local_rows, head_width = queries.shape
    first_device = lax.axis_index("ctx") == 0
    query_unit = unit_rows(queries.astype(jnp.float32))
    key_unit = unit_rows(keys.astype(jnp.float32))
    query_half = query_unit.astype(jnp.bfloat16)
    key_half = key_unit.astype(jnp.bfloat16)
    tails = jnp.stack([key_half[:, local_rows - WINDOW :], values[:, local_rows - WINDOW :]])
    prior = passed_along(tails, "ctx", 1)
    gate_now = w_gate[0]
    up_now = w_up[0]
    down_now = w_down[0]
    mixed = []
    for group_at in range(group_count):
        if group_at == 0:
            halo_rows = prior[:, 0]
            masked_head = first_device
        else:
            halo_rows = jnp.where(first_device, prior[:, group_at - 1], prior[:, group_at])
            masked_head = None
        ext_keys = jnp.concatenate([halo_rows[0], key_half[group_at]], axis=0)
        ext_values = jnp.concatenate([halo_rows[1], values[group_at]], axis=0)
        attended = band_attention(query_half[group_at], ext_keys, ext_values, masked_head)
        grads = fast_grads(
            key_unit[group_at],
            values[group_at].astype(jnp.float32),
            rates[0, group_at],
            gate_now,
            up_now,
            down_now,
        )
        ortho = orthogonal(lax.psum(grads, "ctx"))
        gate_now = gate_now + step_size * ortho[0]
        up_now = up_now + step_size * ortho[1]
        down_now = down_now + step_size * ortho[2].T
        fast_out = apply_fast(query_unit[group_at], gate_now, up_now, down_now)
        normed = (
            fast_out
            * lax.rsqrt(jnp.mean(fast_out * fast_out, axis=-1, keepdims=True) + 1e-05)
            * gains[0]
        )
        mixed.append((attended + normed).astype(jnp.bfloat16))
    combined = jnp.stack(mixed)
    proj_columns = lax.all_to_all(out_proj, "head", split_axis=1, concat_axis=0, tiled=True)
    summed = jnp.einsum(
        "ctf,fo->cto",
        lax.all_gather(combined, "head", axis=2, tiled=True),
        proj_columns,
        preferred_element_type=jnp.float32,
    )
    return summed.astype(jnp.bfloat16)


def solution(mesh):
    return jax.shard_map(
        body,
        mesh=mesh,
        in_specs=(
            P(None, "ctx", "head"),
            P(None, "ctx", "head"),
            P(None, "ctx", "head"),
            P("head", None, "ctx"),
            P("head", None, None),
            P("head", None, None),
            P("head", None, None),
            P("head", None),
            P("head", None),
        ),
        out_specs=P(None, "ctx", "head"),
        check_vma=False,
    )
```

profile of v0, /device:TPU:1, one launch (start us, length us, event | category | flops | bytes accessed | tf_op | source)
XLA Modules:
  0.0 370.9 jit_solution(8970687296122975035)
XLA Ops:
  6.5 1.3 fusion.18
  7.9 1.2 convert_divide_fusion
  10.1 3.6 collective-permute-start
  16.8 1.3 convolution_bitcast_fusion.4
  18.1 1.4 convolution_bitcast_fusion.5
  19.5 1.4 convolution_bitcast_fusion.3
  20.9 1.3 pad_maximum_fusion
  23.4 1.3 fusion.17
  29.7 1.6 slice_bitcast_fusion.28
  31.4 2.0 fusion.127
  33.4 82.0 %all-reduce.3.cloned.1.call-done = f32[3,256,512]{2,1,0:T(8,128)} async-done(((f32[3,256,512]{2,1,0:T(8,128)}), f32[3,256,512]{2,1,0:T(8,128)}) %all-reduce.3.cloned.1.call-update) | async-done | bytes 1572880 | tf_op jit(solution)/shard_map/psum | solution.py:116
  115.4 1.8 multiply_reduce_fusion.1
  117.3 1.8 fusion.85
  120.1 1.8 multiply_add_fusion.9
  121.9 1.7 fusion.128
  124.5 1.6 multiply_add_fusion.8
  126.1 1.8 fusion.129
  128.9 1.6 multiply_add_fusion.7
  130.4 1.7 fusion.130
  133.0 1.6 multiply_add_fusion.6
  134.6 1.7 fusion.131
  137.2 1.6 multiply_add_fusion.5
  139.9 1.5 fusion.54
  142.5 1.3 convolution_bitcast_fusion.1
  143.8 1.4 convolution_bitcast_fusion.2
  145.2 1.4 convolution_bitcast_fusion
  146.6 1.3 pad_maximum_fusion.1
  149.0 2.0 fusion.126
  153.2 1.9 multiply_reduce_fusion.3
  155.1 2.0 copy.11
  157.1 2.8 fusion.16
  159.9 83.1 %all-reduce.5.cloned.1.call-done = f32[3,256,512]{2,1,0:T(8,128)} async-done(((f32[3,256,512]{2,1,0:T(8,128)}), f32[3,256,512]{2,1,0:T(8,128)}) %all-reduce.5.cloned.1.call-update) | async-done | bytes 1572880 | tf_op jit(solution)/shard_map/psum | solution.py:116
  243.0 1.8 multiply_reduce_fusion
  244.9 1.8 fusion.86
  247.6 1.8 multiply_add_fusion.4
  249.4 1.7 fusion.132
  252.1 1.8 multiply_add_fusion.3
  253.8 1.7 fusion.133
  256.4 1.6 multiply_add_fusion.2
  258.0 1.7 fusion.134
  260.6 1.6 multiply_add_fusion.1
  262.2 1.7 fusion.135
  264.8 1.8 multiply_add_fusion
  267.7 1.2 convolution_multiply_fusion
  270.3 2.0 fusion.15
  273.4 43.4 %all_to_all.19 = bf16[256,16,256]{2,0,1:T(8,128)(2,1)S(1)} all-to-all(bf16[256,16,256]{2,0,1:T(8,128)(2,1)S(1)} %bitcast.208), channel_id=1, replica_groups=mesh['ctx'=8,'head'=16] {'head'}, dimensions={1} | all-to-all | bytes 4194304 | tf_op jit(solution)/shard_map/all_to_all | solution.py:128
  316.9 40.8 %all-gather.2.cloned.1.call-done = bf16[2,512,4096]{2,1,0:T(8,128)(2,1)} async-done(((bf16[2,512,256]{2,1,0:T(8,128)(2,1)}), bf16[2,512,4096]{2,1,0:T(8,128)(2,1)}) %all-gather.2.cloned.1.call-update) | async-done | bytes 8388624 | tf_op jit(solution)/shard_map/all_gather | solution.py:131
  357.6 6.5 %convolution_convert_fusion = bf16[2,512,256]{2,1,0:T(8,128)(2,1)} fusion(bf16[2,512,4096]{2,1,0:T(8,128)(2,1)} %all-gather.2.cloned.1.call-done, bf16[4096,256,1]{1,0,2:T(8,128)(2,1)S(1)} %bitcast.210), kind=kOutput, calls=%fused_computation.29 | convolution fusion | flops 2147745792 | bytes 11010048 | tf_op jit(solution)/shard_map/ctf,fo->cto/dot_general | solution.py:129
  (92 shorter events, 28.8 us)
Async XLA Ops:
  6.5 2.6 copy-start.5
  6.5 108.9 %all-reduce.3.cloned.1.call-start = ((), (), s32[]{:S(2)}) async-start(), calls=%async_computation.1 | async-start | bytes 3145728 | tf_op jit(solution)/shard_map/psum | solution.py:116
  9.1 4.5 %copy-start.21 = (f32[1,2,512]{2,1,0:T(2,128)S(1)}, f32[1,2,512]{2,1,0:T(2,128)}, u32[]{:S(2)}) copy-start(f32[1,2,512]{2,1,0:T(2,128)} %param.12) | copy-start | bytes 12292
  9.1 4.5 %copy-start = (f32[1,256,512]{2,1,0:T(8,128)S(1)}, f32[1,256,512]{2,1,0:T(8,128)}, u32[]{:S(2)}) copy-start(f32[1,256,512]{2,1,0:T(8,128)} %param.13) | copy-start | bytes 1572868
  9.2 5.5 %copy-start.8 = (f32[1,256,512]{2,1,0:T(8,128)S(1)}, f32[1,256,512]{2,1,0:T(8,128)}, u32[]{:S(2)}) copy-start(f32[1,256,512]{2,1,0:T(8,128)} %param.14) | copy-start | bytes 1572868
  10.1 17.9 %collective-permute-start = (bf16[2,2,256,256]{3,2,1,0:T(8,128)(2,1)}, bf16[2,2,256,256]{3,2,1,0:T(8,128)(2,1)}, u32[]{:S(2)}, u32[]{:S(2)}) collective-permute-start(bf16[2,2,256,256]{3,2,1,0:T(8,128)(2,1)} %pad_maximum_fusion.2), channel_id=1, source_target_pairs={{0,16},{16,32},{32,48},{48,64},{64,80},{80,96},{96,112},{112,0},{1... | collective-permute-start | bytes 1572872 | tf_op jit(solution)/shard_map/ppermute | solution.py:19
  14.7 1.0 copy-start.11
  22.1 2.7 copy-start.12
  22.2 220.8 %all-reduce.5.cloned.1.call-start = ((), (), s32[]{:S(2)}) async-start(), calls=%async_computation.2 | async-start | bytes 3145728 | tf_op jit(solution)/shard_map/psum | solution.py:116
  23.4 3.1 copy-start.13
  27.8 5.6 %copy-start.16 = (bf16[2,512,256]{2,1,0:T(8,128)(2,1)}, bf16[2,512,256]{2,1,0:T(8,128)(2,1)S(1)}, u32[]{:S(2)}) copy-start(bf16[2,512,256]{2,1,0:T(8,128)(2,1)S(1)} %get-tuple-element.6) | copy-start | bytes 1572868
  115.4 1.9 copy-start.14
  138.8 1.1 copy-start.9
  139.9 1.5 copy-start.1
  139.9 1.5 copy-start.6
  147.8 1.0 copy-start.17
  147.8 1.1 copy-start.18
  147.8 1.1 copy-start.20
  147.9 209.8 %all-gather.2.cloned.1.call-start = ((), (), s32[]{:S(2)}) async-start(), calls=%async_computation.3 | async-start | bytes 8912896 | tf_op jit(solution)/shard_map/all_gather | solution.py:131
  149.0 2.0 copy-start.3
  150.9 1.1 copy-start.10
  152.0 1.2 copy-start.2
  153.2 3.9 %copy-start.22 = (f32[1,256]{1,0:T(1,128)S(1)}, f32[1,256]{1,0:T(1,128)}, u32[]{:S(2)}) copy-start(f32[1,256]{1,0:T(1,128)} %param.16) | copy-start | bytes 3076
  243.0 1.9 copy-start.15
  264.8 1.8 copy-start.4
  270.3 2.0 copy-start.19
  270.3 2.9 copy-start.7
Sparse Core Ops, SparseCore 0:
  22.3 93.0 all-reduce.2
  148.0 94.9 all-reduce.4
  273.3 84.2 all-gather.1
where the time goes:
time: 377 us; the launch traced here: 371 us
  waiting for transfers between devices  206 us (55%)
  matrix products  80.6 us (21%)
  blocking collectives  43.4 us (12%)
  other arithmetic  14 us (4%)
  between operations  14 us (4%)
  local copies, waits for them, and re-layouts  8.64 us (2%)
  starting transfers between devices  4.11 us (1%)
    psum x2, waiting for transfers between devices, body(): ortho = orthogonal(lax.psum(grads, 'ctx'))  165 us
    all_to_all x1, blocking collectives, body(): lax.all_to_all(out_proj, 'head', split_axis=1, concat_axis=0, tiled=True)  43.4 us
    all_gather x1, waiting for transfers between devices, body(): lax.all_gather(combined, 'head', axis=2, tiled=True)  40.8 us
    dot_general x18, matrix products, exact_dot(): jnp.dot(left, right, precision=highest, preferred_element_type=jnp.float32)  22.3 us
    dot_general x10, matrix products, orthogonal(): gram = jnp.einsum('mik,mjk->mij', iterate, iterate, precision=highest)  17 us
    dot_general x10, matrix products, quintic_step(): jnp.einsum('mij,mjk->mik', poly, iterate, precision=highest)  16.6 us
    dot_general x10, matrix products, quintic_step(): jnp.einsum('mij,mjk->mik', gram, gram, precision=highest)  9.34 us
  transfers between devices with their start and end apart: 4, of which 4 were waited for; matrix products, arithmetic and copies ran while one was open for 8% of the time, Pallas kernels for 0%

commit v1 on v0

--- a/solution.py
+++ b/solution.py
@@ -128,7 +128,12 @@
     proj_columns = lax.all_to_all(out_proj, "head", split_axis=1, concat_axis=0, tiled=True)
     summed = jnp.einsum(
         "ctf,fo->cto",
-        lax.all_gather(combined, "head", axis=2, tiled=True),
+        jnp.concatenate(
+            jax.lax.all_to_all(
+                jnp.stack(jax.lax.axis_size("head") * [combined], axis=0), "head", 0, 0
+            ),
+            axis=2,
+        ),
         proj_columns,
         preferred_element_type=jnp.float32,
     )

time: 377 us -> 415 us (1.10)
  blocking collectives: 43.4 us -> 104 us
  waiting for transfers between devices: 206 us -> 173 us
  local copies, waits for them, and re-layouts: 8.64 us -> 15.6 us
  starting transfers between devices: 4.11 us -> 10.5 us
    all_to_all x1, blocking collectives: 43.4 us -> 104 us  [body(): jax.lax.all_to_all(jnp.stack(jax.lax.axis_size('head') * [combined], axis...]
    all_gather x1 -> x0, waiting for transfers between devices: 40.8 us -> none  [body(): lax.all_gather(combined, 'head', axis=2, tiled=True)]
    psum x2, waiting for transfers between devices: 165 us -> 173 us  [body(): ortho = orthogonal(lax.psum(grads, 'ctx'))]
    all_to_all x0 -> x1, starting transfers between devices: none -> 6.44 us  [body(): lax.all_to_all(out_proj, 'head', split_axis=1, concat_axis=0, tiled=True)]
  transfers between devices with their start and end apart: 4 -> 4, of which waited for: 4 -> 2; matrix products, arithmetic and copies ran while one was open for 8% -> 22% of each run, Pallas kernels for 0% -> 0%
where the time goes in v1:
time: 415 us; the launch traced here: 408 us
  waiting for transfers between devices  173 us (42%)
  blocking collectives  104 us (25%)
  matrix products  78.8 us (19%)
  local copies, waits for them, and re-layouts  15.6 us (4%)
  between operations  14.3 us (3%)
  other arithmetic  12.4 us (3%)
  starting transfers between devices  10.5 us (3%)
    psum x2, waiting for transfers between devices, body(): ortho = orthogonal(lax.psum(grads, 'ctx'))  173 us
    all_to_all x1, blocking collectives, body(): jax.lax.all_to_all(jnp.stack(jax.lax.axis_size('head') * [combined], axis...  104 us
    dot_general x18, matrix products, exact_dot(): jnp.dot(left, right, precision=highest, preferred_element_type=jnp.float32)  22.2 us
    dot_general x10, matrix products, orthogonal(): gram = jnp.einsum('mik,mjk->mij', iterate, iterate, precision=highest)  17.7 us
    dot_general x10, matrix products, quintic_step(): jnp.einsum('mij,mjk->mik', poly, iterate, precision=highest)  16.2 us
    dot_general x10, matrix products, quintic_step(): jnp.einsum('mij,mjk->mik', gram, gram, precision=highest)  9.34 us
  transfers between devices with their start and end apart: 4, of which 2 were waited for; matrix products, arithmetic and copies ran while one was open for 22% of the time, Pallas kernels for 0%

profile of v1, /device:TPU:1, one launch (start us, length us, event | category | flops | bytes accessed | tf_op | source)
XLA Modules:
  0.0 408.1 jit_solution(11108295541599063590)
XLA Ops:
  6.5 1.3 fusion.32
  12.7 1.4 convolution_bitcast_fusion.3
  14.0 1.4 convolution_bitcast_fusion.5
  15.4 1.3 convolution_bitcast_fusion.4
  16.7 1.3 pad_maximum_fusion
  19.0 3.6 collective-permute-start
  22.6 3.3 copy.22
  25.8 2.4 copy.23
  28.2 6.4 %all-to-all-start.1 = ((bf16[256,16,256]{2,0,1:T(8,128)(2,1)}), bf16[256,16,256]{2,0,1:T(8,128)(2,1)}, u32[]{:S(2)}, u32[]{:S(2)}) async-start(bf16[256,16,256]{2,0,1:T(8,128)(2,1)} %copy.23), calls=%async_computation.1 | async-start | bytes 4194304 | tf_op jit(solution)/shard_map/all_to_all | solution.py:128
  39.3 1.3 slice_select_fusion
  41.3 1.6 slice_bitcast_fusion.28
  42.9 2.1 fusion.141
  45.0 89.8 %all-reduce.3.cloned.1.call-done = f32[3,256,512]{2,1,0:T(8,128)} async-done(((f32[3,256,512]{2,1,0:T(8,128)}), f32[3,256,512]{2,1,0:T(8,128)}) %all-reduce.3.cloned.1.call-update) | async-done | bytes 1572880 | tf_op jit(solution)/shard_map/psum | solution.py:116
  134.8 1.8 multiply_reduce_fusion.1
  136.6 1.8 fusion.99
  139.4 1.8 multiply_add_fusion.9
  141.2 1.7 fusion.142
  143.8 1.6 multiply_add_fusion.8
  145.4 1.8 fusion.143
  148.2 1.6 multiply_add_fusion.7
  149.8 1.7 fusion.144
  152.4 1.6 multiply_add_fusion.6
  154.0 1.7 fusion.145
  156.6 1.6 multiply_add_fusion.5
  159.3 1.3 fusion.68
  161.7 1.3 convolution_bitcast_fusion.1
  163.0 1.4 convolution_bitcast_fusion.2
  164.4 1.4 convolution_bitcast_fusion
  165.7 1.3 pad_maximum_fusion.1
  168.2 1.9 fusion.140
  172.4 1.9 multiply_reduce_fusion.3
  174.3 2.0 copy.19
  176.3 2.8 fusion.30
  179.1 83.1 %all-reduce.5.cloned.1.call-done = f32[3,256,512]{2,1,0:T(8,128)} async-done(((f32[3,256,512]{2,1,0:T(8,128)}), f32[3,256,512]{2,1,0:T(8,128)}) %all-reduce.5.cloned.1.call-update) | async-done | bytes 1572880 | tf_op jit(solution)/shard_map/psum | solution.py:116
  262.2 1.8 multiply_reduce_fusion
  264.1 2.3 fusion.100
  267.3 1.8 multiply_add_fusion.4
  269.1 1.7 fusion.146
  271.7 1.6 multiply_add_fusion.3
  273.3 1.7 fusion.147
  275.9 1.6 multiply_add_fusion.2
  277.5 1.8 fusion.148
  280.3 1.6 multiply_add_fusion.1
  281.9 1.7 fusion.149
  284.5 1.6 multiply_add_fusion
  289.8 1.9 fusion.29
  292.7 103.6 %all_to_all.21 = bf16[16,2,512,256]{3,2,1,0:T(8,128)(2,1)S(1)} all-to-all(bf16[16,2,512,256]{3,2,1,0:T(8,128)(2,1)S(1)} %stack.75), channel_id=1, replica_groups=mesh['ctx'=8,'head'=16] {'head'}, dimensions={0} | all-to-all | bytes 16777216 | tf_op jit(solution)/shard_map/all_to_all | solution.py:132
  396.3 4.7 %fusion.12 = bf16[2,512,256]{2,1,0:T(8,128)(2,1)} fusion(bf16[256,16,256]{2,0,1:T(8,128)(2,1)} %all-to-all-done.1, bf16[16,2,512,256]{3,2,1,0:T(8,128)(2,1)S(1)} %all_to_all.21), kind=kOutput, calls=%fused_computation.33 | convolution fusion | flops 2147745792 | bytes 11010048 | tf_op jit(solution)/shard_map/ctf,fo->cto/dot_general | solution.py:129
  (101 shorter events, 30.6 us)
Async XLA Ops:
  6.5 2.6 copy-start
  6.5 128.2 %all-reduce.3.cloned.1.call-start = ((), (), s32[]{:S(2)}) async-start(), calls=%async_computation.2 | async-start | bytes 3145728 | tf_op jit(solution)/shard_map/psum | solution.py:116
  9.1 8.9 %copy-start.6 = (bf16[2,512,256]{2,1,0:T(8,128)(2,1)}, bf16[2,512,256]{2,1,0:T(8,128)(2,1)S(1)}, u32[]{:S(2)}) copy-start(bf16[2,512,256]{2,1,0:T(8,128)(2,1)S(1)} %get-tuple-element.8) | copy-start | bytes 1572868
  9.1 1.2 copy-start.11
  10.4 1.0 copy-start.25
  10.4 1.1 copy-start.8
  10.4 1.2 copy-start.14
  19.0 20.3 %collective-permute-start = (bf16[2,2,256,256]{3,2,1,0:T(8,128)(2,1)}, bf16[2,2,256,256]{3,2,1,0:T(8,128)(2,1)}, u32[]{:S(2)}, u32[]{:S(2)}) collective-permute-start(bf16[2,2,256,256]{3,2,1,0:T(8,128)(2,1)} %pad_maximum_fusion.2), channel_id=1, source_target_pairs={{0,16},{16,32},{32,48},{48,64},{64,80},{80,96},{96,112},{112,0},{1... | collective-permute-start | bytes 1572872 | tf_op jit(solution)/shard_map/ppermute | solution.py:19
  28.2 7.0 %copy-start.7 = (bf16[2,512,256]{2,1,0:T(8,128)(2,1)S(1)}, bf16[2,512,256]{2,1,0:T(8,128)(2,1)}, u32[]{:S(2)}) copy-start(bf16[2,512,256]{2,1,0:T(8,128)(2,1)} %copy-done.6) | copy-start | bytes 1572868
  28.2 7.9 %copy-start.16 = (bf16[2,512,256]{2,1,0:T(8,128)(2,1)S(1)}, bf16[2,512,256]{2,1,0:T(8,128)(2,1)}, u32[]{:S(2)}) copy-start(bf16[2,512,256]{2,1,0:T(8,128)(2,1)} %param.9) | copy-start | bytes 1572868
  28.2 263.5 %all-to-all-start.1 = ((bf16[256,16,256]{2,0,1:T(8,128)(2,1)}), bf16[256,16,256]{2,0,1:T(8,128)(2,1)}, u32[]{:S(2)}, u32[]{:S(2)}) async-start(bf16[256,16,256]{2,0,1:T(8,128)(2,1)} %copy.23), calls=%async_computation.1 | async-start | bytes 4194304 | tf_op jit(solution)/shard_map/all_to_all | solution.py:128
  34.7 1.7 copy-start.15
  34.7 2.7 copy-start.9
  34.7 227.5 %all-reduce.5.cloned.1.call-start = ((), (), s32[]{:S(2)}) async-start(), calls=%async_computation.3 | async-start | bytes 3145728 | tf_op jit(solution)/shard_map/psum | solution.py:116
  38.1 4.8 %copy-start.23 = (bf16[512,256]{1,0:T(8,128)(2,1)S(1)}, bf16[512,256]{1,0:T(8,128)(2,1)}, u32[]{:S(2)}) copy-start(bf16[512,256]{1,0:T(8,128)(2,1)} %get-tuple-element.13) | copy-start | bytes 786436
  39.3 3.6 copy-start.19
  134.8 1.9 copy-start.17
  156.6 1.6 copy-start.1
  158.2 1.1 copy-start.12
  159.2 1.3 copy-start.2
  159.3 1.3 copy-start.10
  167.0 1.0 copy-start.20
  167.0 1.1 copy-start.21
  167.0 1.1 copy-start.24
  168.2 1.9 copy-start.4
  170.1 1.1 copy-start.13
  171.2 1.2 copy-start.3
  172.4 4.0 copy-start.26
  262.2 1.9 copy-start.18
  284.5 1.6 copy-start.5
  289.8 1.9 copy-start.22
Sparse Core Ops, SparseCore 0:
  18.2 116.5 all-reduce.2
  167.2 94.9 all-reduce.4
